TPU v7x, 32 devices: a whole 2x2x4 slice. The times are simulated.
32 devices in a mesh: visit: 4 (over y, x), ccd: 8 (over z, core).
Axes of the slice: x: 2, y: 2, z: 4, core: 2. Of those that a mesh axis runs over, the one named last changes fastest.
Arguments:
- exposure: bfloat16 [4, 512, 4096], P('visit', 'ccd'), may hold values from -6 to 6
- offsets: int32 [4, 8, 2], P('visit', 'ccd'), may hold values from -32 to 32
- fraction: float32 [4, 8, 2], P('visit', 'ccd'), may hold values from 0 to 1
- route_patch: int32 [4, 512], P('visit', 'ccd'), may hold values from 0 to 31, as said below
- route_slot: int32 [4, 512], P('visit', 'ccd'), may hold values from 0 to 63
- block_weight: bfloat16 [4, 512], P('visit', 'ccd'), may hold values from 0.25 to 4
- kernel_rows: float32 [33], replicated, may hold values from -1 to 1
- kernel_columns: float32 [33], replicated, may hold values from -1 to 1
Outputs:
- coadded: bfloat16 [512, 16384], P('visit', 'ccd')
- matched: float32 [512, 16384], P('visit', 'ccd')
Inputs may be any that keep to these rules, and one draw needn't show every extreme that they name: `route_patch`: no patch is named by more than 8 of one exposure's 64 blocks; one patch, drawn from the seed, is named by exactly 8 blocks of every exposure.
All inputs are finite; a program needn't handle non-finite values.
Results may differ from a plain program's by a relative error of at most 0.0082.
Values may be sent and summed in bfloat16 or wider, within the bound.
No kernel may reach another device: no remote copies, remote signals or barrier semaphores. Data moves between devices by JAX's collectives and lax.ppermute only.
A program may use at most 64 MiB of HBM per device.

v0:
```python
import jax
import jax.numpy as jnp
from jax import lax
from jax.sharding import PartitionSpec as P

BLOCK_ROWS = 32
BLOCK_COLS = 128
MARGIN = 40
HALF_KERNEL = 16


def extended_2(x, sides, width):
    for axis, dim in sides:
        devices, length = (lax.axis_size(axis), x.shape[dim])
        up = [(i, (i + 1) % devices) for i in range(devices - 1)]
        down = [(j, i) for i, j in up]
        last = lax.slice_in_dim(x, length - width, length, axis=dim)
        first = lax.slice_in_dim(x, 0, width, axis=dim)
        before = lax.ppermute(last, axis, up)
        after = lax.ppermute(first, axis, down)
        x = jnp.concatenate([before, x, after], axis=dim)
    return x


def lanczos_weights(fraction_part):
    distance = jnp.arange(3, -3, -1).astype(jnp.float32) - fraction_part
    kernel = jnp.sinc(distance) * jnp.sinc(distance / 3.0)
    return (kernel / jnp.sum(kernel)).astype(jnp.bfloat16)


def band_matrix(out_count, in_count, first_lag, weights):
    lag_index = jnp.arange(in_count)[None, :] - jnp.arange(out_count)[:, None] - first_lag
    matrix = jnp.zeros((out_count, in_count), jnp.bfloat16)
    for position in range(weights.shape[0]):
        matrix = jnp.where(lag_index == position, weights[position], matrix)
    return matrix


def column_pass(pixels, window_matrix, rim_width):
    tile_rows = pixels.shape[0]
    widened = jnp.pad(pixels, ((0, 0), (128 - rim_width, 128 - rim_width)))
    block_count = widened.shape[1] // 128 - 2
    blocked = widened.reshape(tile_rows, block_count + 2, 128)
    summed = jnp.zeros((tile_rows, block_count, 128), jnp.float32)
    for part_index in range(3):
        summed = summed + jnp.einsum(
            "rjb,bo->rjo",
            blocked[:, part_index : part_index + block_count],
            window_matrix[128 * part_index : 128 * (part_index + 1)],
            preferred_element_type=jnp.float32,
        )
    return summed.reshape(tile_rows, block_count * 128)


def on_device(
    exposure, offsets, fraction, route_patch, route_slot, block_weight, kernel_rows, kernel_columns
):
    pixel_tile = exposure[0]
    tile_rows, tile_columns = pixel_tile.shape
    extended = extended_2(pixel_tile, (("ccd", 0),), MARGIN)
    row_weights = lanczos_weights(fraction[0, 0, 0])
    column_weights = lanczos_weights(fraction[0, 0, 1])
    row_matrix = band_matrix(
        tile_rows, tile_rows + 2 * MARGIN, MARGIN - offsets[0, 0, 0] - 3, row_weights
    )
    row_warped = jnp.dot(row_matrix, extended, preferred_element_type=jnp.float32).astype(
        jnp.bfloat16
    )
    column_matrix = band_matrix(128, 384, 125 - offsets[0, 0, 1], column_weights).T
    warped = column_pass(row_warped, column_matrix, 0).astype(jnp.bfloat16)
    blocks = warped.reshape(
        tile_rows // BLOCK_ROWS, BLOCK_ROWS, tile_columns // BLOCK_COLS, BLOCK_COLS
    )
    blocks = blocks.transpose(0, 2, 1, 3).reshape(-1, BLOCK_ROWS * BLOCK_COLS)
    block_count = blocks.shape[0]
    visit_count = lax.axis_size("visit")
    owner_count = visit_count * lax.axis_size("ccd")
    capacity = 4 * block_count // owner_count
    destination = route_patch[0]
    block_order = jnp.arange(block_count)
    same_before = (destination[None, :] == destination[:, None]) & (
        block_order[None, :] < block_order[:, None]
    )
    block_rank = jnp.sum(same_before.astype(jnp.int32), axis=1)
    position = destination * capacity + block_rank
    placement = (jnp.arange(owner_count * capacity)[:, None] == position[None, :]).astype(
        jnp.bfloat16
    )
    slot_table = jnp.where(
        route_slot[0][:, None] == jnp.arange(block_count)[None, :],
        block_weight[0][:, None],
        jnp.zeros((), jnp.bfloat16),
    )
    send_pixels = jnp.dot(placement, blocks, preferred_element_type=jnp.float32).astype(
        jnp.bfloat16
    )
    send_weights = jnp.dot(placement, slot_table, preferred_element_type=jnp.float32).astype(
        jnp.bfloat16
    )
    got_pixels, got_weights = (
        lax.all_to_all(
            send_pixels.reshape(owner_count, capacity, BLOCK_ROWS * BLOCK_COLS),
            ("visit", "ccd"),
            split_axis=0,
            concat_axis=0,
            tiled=True,
        ),
        lax.all_to_all(
            send_weights.reshape(owner_count, capacity, block_count),
            ("visit", "ccd"),
            split_axis=0,
            concat_axis=0,
            tiled=True,
        ),
    )
    got_pixels = got_pixels.reshape(-1, BLOCK_ROWS * BLOCK_COLS)
    got_weights = got_weights.reshape(-1, block_count)
    numerator = lax.dot_general(
        got_weights, got_pixels, (((0,), (0,)), ((), ())), preferred_element_type=jnp.float32
    )
    weight_total = jnp.sum(got_weights.astype(jnp.float32), axis=0)
    slot_values = (numerator / jnp.maximum(weight_total, 1.0)[:, None]).astype(jnp.bfloat16)
    patch_rows = 2 * tile_rows
    patch_columns = tile_columns // 2
    coadded = slot_values.reshape(
        patch_rows // BLOCK_ROWS, patch_columns // BLOCK_COLS, BLOCK_ROWS, BLOCK_COLS
    )
    coadded = coadded.transpose(0, 2, 1, 3).reshape(patch_rows, patch_columns)
    row_kernel = kernel_rows.astype(jnp.bfloat16)
    column_kernel = kernel_columns.astype(jnp.bfloat16)
    row_filter = band_matrix(patch_rows, patch_rows + 2 * HALF_KERNEL, 0, row_kernel)
    column_filter = band_matrix(128, 384, 128 - HALF_KERNEL, column_kernel).T
    framed = extended_2(coadded, (("visit", 0), ("ccd", 1)), HALF_KERNEL)
    smoothed = jnp.dot(row_filter, framed, preferred_element_type=jnp.float32).astype(jnp.bfloat16)
    matched = column_pass(smoothed, column_filter, HALF_KERNEL)
    return (coadded, matched)


def solution(mesh):
    placed = (
        P("visit", "ccd", None),
        P("visit", "ccd", None),
        P("visit", "ccd", None),
        P("visit", "ccd"),
        P("visit", "ccd"),
        P("visit", "ccd"),
        P(),
        P(),
    )
    return jax.shard_map(
        on_device,
        mesh=mesh,
        in_specs=placed,
        out_specs=(P("visit", "ccd"), P("visit", "ccd")),
        check_vma=False,
    )
```

profile of v0, /device:TPU:1, one launch (start us, length us, event | category | flops | bytes accessed | tf_op | source)
XLA Modules:
  0.0 138.1 jit_solution(13725084230487260575)
XLA Ops:
  0.6 1.1 slice_bitcast_fusion.1
  1.8 4.6 %collective-permute-start = (bf16[40,4096]{1,0:T(8,128)(2,1)S(1)}, bf16[40,4096]{1,0:T(8,128)(2,1)S(1)}, u32[]{:S(2)}, u32[]{:S(2)}) collective-permute-start(bf16[40,4096]{1,0:T(8,128)(2,1)S(1)} %get-tuple-element.15), channel_id=1, source_target_pairs={{0,1},{1,2},{2,3},{3,4},{4,5},{5,6},{6,7},{8,9},{9,10},{10,11},{11... | collective-permute-start | bytes 983048 | tf_op jit(solution)/shard_map/ppermute | solution.py:19
  6.3 1.9 %collective-permute-start.1 = (bf16[40,4096]{1,0:T(8,128)(2,1)S(1)}, bf16[40,4096]{1,0:T(8,128)(2,1)S(1)}, u32[]{:S(2)}, u32[]{:S(2)}) collective-permute-start(bf16[40,4096]{1,0:T(8,128)(2,1)S(1)} %get-tuple-element.16), channel_id=1, source_target_pairs={{1,0},{2,1},{3,2},{4,3},{5,4},{6,5},{7,6},{9,8},{10,9},{11,10},{12... | collective-permute-start | bytes 983048 | tf_op jit(solution)/shard_map/ppermute | solution.py:20
  8.3 0.9 convert_reduce_fusion.1
  9.2 0.7 fusion.272
  9.8 0.9 convolution_convert_fusion.3
  10.8 0.1 copy.44
  10.9 0.7 reshape.62
  11.6 6.1 %all-to-all-start = ((bf16[32,2,256]{2,1,0:T(2,128)(2,1)}), bf16[32,2,256]{2,1,0:T(2,128)(2,1)S(1)}, u32[]{:S(2)}, u32[]{:S(2)}) async-start(bf16[32,2,256]{2,1,0:T(2,128)(2,1)} %reshape.62), calls=%async_computation | async-start | bytes 65536 | tf_op jit(solution)/shard_map/all_to_all | solution.py:108
  17.8 1.4 %fusion.337 = (f32[1,1,1]{2,1,0:T(1,128)}, f32[1,1,1]{2,1,0:T(1,128)}) fusion(f32[1,1,2]{2,1,0:T(1,128)} %param.11), kind=kLoop, calls=%fused_computation.405 | loop fusion | bytes 16 | tf_op jit(solution)/shard_map/slice | solution.py:62
  19.2 1.3 fusion.286
  20.5 1.3 divide_convert_fusion.1
  21.8 0.7 fusion.339
  22.4 1.3 fusion.338
  23.8 1.3 fusion.285
  26.3 1.3 divide_convert_fusion
  27.6 0.7 fusion.336
  28.3 3.9 %fusion.57 = bf16[384,128]{1,0:T(8,128)(2,1)S(1)} fusion(s32[]{:T(128)} %bitcast.17, bf16[]{:T(256)} %bitcast.24, bf16[]{:T(256)} %bitcast.23, bf16[]{:T(256)} %bitcast.22, bf16[]{:T(256)} %bitcast.21, bf16[]{:T(256)} %bitcast.20, bf16[]{:T(256)} %bitcast.19), kind=kLoop, calls=%fused_computation.71 | loop fusion | flops 688128 | bytes 98320 | tf_op jit(solution)/shard_map/jit(_where)/select_n | solution.py:35
  32.2 0.0 collective-permute-done
  32.2 0.0 collective-permute-done.1
  32.2 5.0 %convolution_convert_fusion.1 = bf16[64,4096]{1,0:T(8,128)(2,1)S(1)} fusion(bf16[40,4096]{1,0:T(8,128)(2,1)S(1)} %collective-permute-done.1, bf16[64,4096]{1,0:T(8,128)(2,1)} %bitcast.164, bf16[40,4096]{1,0:T(8,128)(2,1)S(1)} %collective-permute-done, s32[]{:T(128)} %bitcast.6, bf16[]{:T(256)} %bitcast.13, bf16[]{:T(256)} %bitcast.12, bf16[]{:T(256)} %bitcast.11, ...), kind=kOutput, calls=%fused_computation.3 | convolution fusion | flops 79427584 | bytes 1703952 | tf_op jit(solution)/shard_map/dot_general | solution.py:66
  37.2 0.3 reshape.48
  37.5 0.3 fusion.14
  37.8 0.3 convolution_add_fusion.3
  38.1 0.3 fusion.3
  38.4 0.2 copy.45
  38.6 2.0 %fusion = bf16[32,8,4096]{2,1,0:T(8,128)(2,1)} fusion(bf16[8,8,32,128]{3,2,1,0:T(8,128)(2,1)S(1)} %bitcast.163, s32[64]{0:T(128)S(1)} %fusion.272), kind=kOutput, calls=%fused_computation.1 | convolution fusion | flops 135282688 | bytes 2621696 | tf_op jit(solution)/shard_map/dot_general | solution.py:94
  40.7 0.0 copy-start.1
  40.7 0.0 copy-start.2
  40.7 0.0 all-to-all-done
  40.7 5.8 %all-to-all-start.1 = ((bf16[32,8,4096]{2,1,0:T(8,128)(2,1)}), bf16[32,8,4096]{2,1,0:T(8,128)(2,1)S(1)}, u32[]{:S(2)}, u32[]{:S(2)}) async-start(bf16[32,8,4096]{2,1,0:T(8,128)(2,1)} %fusion), calls=%async_computation.1 | async-start | bytes 4194304 | tf_op jit(solution)/shard_map/all_to_all | solution.py:101
  46.5 0.0 copy-done.1
  46.5 0.0 copy-done.2
  46.6 0.7 fusion.332
  47.3 0.7 fusion.333
  48.0 20.9 %fusion.63 = bf16[384,128]{1,0:T(8,128)(2,1)S(1)} fusion(bf16[]{:T(256)} %bitcast.99, bf16[]{:T(256)} %bitcast.98, bf16[]{:T(256)} %bitcast.97, bf16[]{:T(256)} %bitcast.96, bf16[]{:T(256)} %bitcast.95, bf16[]{:T(256)} %bitcast.94, bf16[]{:T(256)} %bitcast.93, bf16[]{:T(256)} %bitcast.92, bf16[]{:T(256)} %bitcast.91, bf16[]{:T(256)} %bitcast.90, ...), kind=kLoop, calls=%fused_computation.77 | loop fusion | flops 3342336 | bytes 98370 | tf_op jit(solution)/shard_map/jit(_where)/select_n | solution.py:35
  68.9 0.1 reshape.63
  69.0 0.1 convert_reduce_fusion
  69.1 27.0 %all-to-all-done.1 = bf16[32,8,4096]{2,1,0:T(8,128)(2,1)S(1)} async-done(((bf16[32,8,4096]{2,1,0:T(8,128)(2,1)}), bf16[32,8,4096]{2,1,0:T(8,128)(2,1)S(1)}, u32[]{:S(2)}, u32[]{:S(2)}) %all-to-all-start.1) | async-done | bytes 2097184 | tf_op jit(solution)/shard_map/all_to_all | solution.py:101
  96.1 0.5 fusion.4
  96.6 0.1 copy.64
  96.7 0.2 copy.46
  96.9 0.1 copy.73
  97.1 0.0 copy-start
  97.1 2.8 %collective-permute-start.2 = (bf16[16,2048]{1,0:T(8,128)(2,1)S(1)}, bf16[16,2048]{1,0:T(8,128)(2,1)S(1)}, u32[]{:S(2)}, u32[]{:S(2)}) collective-permute-start(bf16[16,2048]{1,0:T(8,128)(2,1)S(1)} %get-tuple-element.14), channel_id=1, source_target_pairs={{0,8},{8,16},{16,24},{1,9},{9,17},{17,25},{2,10},{10,18},{18,26},{... | collective-permute-start | bytes 196616 | tf_op jit(solution)/shard_map/ppermute | solution.py:19
  99.9 0.7 fusion.334
  100.7 1.3 collective-permute-start.3
  102.0 0.0 collective-permute-done.2
  102.0 0.1 constant_dynamic-update-slice_fusion.1
  102.1 4.3 %collective-permute-done.3 = bf16[16,2048]{1,0:T(8,128)(2,1)S(1)} collective-permute-done((bf16[16,2048]{1,0:T(8,128)(2,1)S(1)}, bf16[16,2048]{1,0:T(8,128)(2,1)S(1)}, u32[]{:S(2)}, u32[]{:S(2)}) %collective-permute-start.3) | collective-permute-done | bytes 65568 | tf_op jit(solution)/shard_map/ppermute | solution.py:20
  106.4 0.1 fusion.330
  106.5 1.9 %collective-permute-start.4 = (bf16[160,16]{1,0:T(8,128)(2,1)S(1)}, bf16[160,16]{1,0:T(8,128)(2,1)S(1)}, u32[]{:S(2)}, u32[]{:S(2)}) collective-permute-start(bf16[160,16]{1,0:T(8,128)(2,1)S(1)} %get-tuple-element.12), channel_id=1, source_target_pairs={{0,1},{1,2},{2,3},{3,4},{4,5},{5,6},{6,7},{8,9},{9,10},{10,11},{11... | collective-permute-start | bytes 15368 | tf_op jit(solution)/shard_map/ppermute | solution.py:19
  108.4 2.4 %collective-permute-start.5 = (bf16[160,16]{1,0:T(8,128)(2,1)S(1)}, bf16[160,16]{1,0:T(8,128)(2,1)S(1)}, u32[]{:S(2)}, u32[]{:S(2)}) collective-permute-start(bf16[160,16]{1,0:T(8,128)(2,1)S(1)} %get-tuple-element.11), channel_id=1, source_target_pairs={{1,0},{2,1},{3,2},{4,3},{5,4},{6,5},{7,6},{9,8},{10,9},{11,10},{12... | collective-permute-start | bytes 15368 | tf_op jit(solution)/shard_map/ppermute | solution.py:20
  110.8 0.7 fusion.335
  111.5 0.0 collective-permute-done.4
  111.5 2.2 %collective-permute-done.5 = bf16[160,16]{1,0:T(8,128)(2,1)S(1)} collective-permute-done((bf16[160,16]{1,0:T(8,128)(2,1)S(1)}, bf16[160,16]{1,0:T(8,128)(2,1)S(1)}, u32[]{:S(2)}, u32[]{:S(2)}) %collective-permute-start.5) | collective-permute-done | bytes 5152 | tf_op jit(solution)/shard_map/ppermute | solution.py:20
  113.7 0.7 concatenate.11
  114.5 21.2 %convolution_convert_fusion.2 = bf16[128,2080]{0,1:T(8,128)(2,1)S(1)} fusion(bf16[160,2080]{1,0:T(8,128)(2,1)S(1)} %concatenate.11, bf16[]{:T(256)} %bitcast.65, bf16[]{:T(256)} %bitcast.64, bf16[]{:T(256)} %bitcast.63, bf16[]{:T(256)} %bitcast.62, bf16[]{:T(256)} %bitcast.61, bf16[]{:T(256)} %bitcast.60, bf16[]{:T(256)} %bitcast.59, bf16[]{:T(256)} %bitcast.58, ...), kind=kOutput, calls=%fused_computation.6 | convolution fusion | flops 86835200 | bytes 1198146 | tf_op jit(solution)/shard_map/dot_general | solution.py:134
  135.7 0.0 copy-done
  135.8 0.3 fusion.211
  136.1 0.3 convolution_add_fusion.1
  136.5 0.3 convolution_add_fusion
  136.8 1.3 copy.53
  (9 shorter events, 0.2 us)
Async XLA Ops:
  1.8 30.4 %collective-permute-start = (bf16[40,4096]{1,0:T(8,128)(2,1)S(1)}, bf16[40,4096]{1,0:T(8,128)(2,1)S(1)}, u32[]{:S(2)}, u32[]{:S(2)}) collective-permute-start(bf16[40,4096]{1,0:T(8,128)(2,1)S(1)} %get-tuple-element.15), channel_id=1, source_target_pairs={{0,1},{1,2},{2,3},{3,4},{4,5},{5,6},{6,7},{8,9},{9,10},{10,11},{11... | collective-permute-start | bytes 983048 | tf_op jit(solution)/shard_map/ppermute | solution.py:19
  6.3 25.8 %collective-permute-start.1 = (bf16[40,4096]{1,0:T(8,128)(2,1)S(1)}, bf16[40,4096]{1,0:T(8,128)(2,1)S(1)}, u32[]{:S(2)}, u32[]{:S(2)}) collective-permute-start(bf16[40,4096]{1,0:T(8,128)(2,1)S(1)} %get-tuple-element.16), channel_id=1, source_target_pairs={{1,0},{2,1},{3,2},{4,3},{5,4},{6,5},{7,6},{9,8},{10,9},{11,10},{12... | collective-permute-start | bytes 983048 | tf_op jit(solution)/shard_map/ppermute | solution.py:20
  11.6 29.0 %all-to-all-start = ((bf16[32,2,256]{2,1,0:T(2,128)(2,1)}), bf16[32,2,256]{2,1,0:T(2,128)(2,1)S(1)}, u32[]{:S(2)}, u32[]{:S(2)}) async-start(bf16[32,2,256]{2,1,0:T(2,128)(2,1)} %reshape.62), calls=%async_computation | async-start | bytes 65536 | tf_op jit(solution)/shard_map/all_to_all | solution.py:108
  40.7 5.9 %copy-start.1 = (f32[33]{0:T(128)S(1)}, f32[33]{0:T(128)}, u32[]{:S(2)}) copy-start(f32[33]{0:T(128)} %param.15) | copy-start | bytes 400
  40.7 5.9 %copy-start.2 = (f32[33]{0:T(128)S(1)}, f32[33]{0:T(128)}, u32[]{:S(2)}) copy-start(f32[33]{0:T(128)} %param.16) | copy-start | bytes 400
  40.7 55.4 %all-to-all-start.1 = ((bf16[32,8,4096]{2,1,0:T(8,128)(2,1)}), bf16[32,8,4096]{2,1,0:T(8,128)(2,1)S(1)}, u32[]{:S(2)}, u32[]{:S(2)}) async-start(bf16[32,8,4096]{2,1,0:T(8,128)(2,1)} %fusion), calls=%async_computation.1 | async-start | bytes 4194304 | tf_op jit(solution)/shard_map/all_to_all | solution.py:101
  97.1 38.6 %copy-start = (bf16[16,8,16,128]{3,1,2,0:T(8,128)(2,1)}, bf16[16,8,16,128]{3,1,2,0:T(8,128)(2,1)S(1)}, u32[]{:S(2)}) copy-start(bf16[16,8,16,128]{3,1,2,0:T(8,128)(2,1)S(1)} %copy.73) | copy-start | bytes 1572868
  97.1 4.8 %collective-permute-start.2 = (bf16[16,2048]{1,0:T(8,128)(2,1)S(1)}, bf16[16,2048]{1,0:T(8,128)(2,1)S(1)}, u32[]{:S(2)}, u32[]{:S(2)}) collective-permute-start(bf16[16,2048]{1,0:T(8,128)(2,1)S(1)} %get-tuple-element.14), channel_id=1, source_target_pairs={{0,8},{8,16},{16,24},{1,9},{9,17},{17,25},{2,10},{10,18},{18,26},{... | collective-permute-start | bytes 196616 | tf_op jit(solution)/shard_map/ppermute | solution.py:19
  100.7 5.7 %collective-permute-start.3 = (bf16[16,2048]{1,0:T(8,128)(2,1)S(1)}, bf16[16,2048]{1,0:T(8,128)(2,1)S(1)}, u32[]{:S(2)}, u32[]{:S(2)}) collective-permute-start(bf16[16,2048]{1,0:T(8,128)(2,1)S(1)} %get-tuple-element.13), channel_id=1, source_target_pairs={{8,0},{16,8},{24,16},{9,1},{17,9},{25,17},{10,2},{18,10},{26,18},{... | collective-permute-start | bytes 196616 | tf_op jit(solution)/shard_map/ppermute | solution.py:20
  106.5 5.0 %collective-permute-start.4 = (bf16[160,16]{1,0:T(8,128)(2,1)S(1)}, bf16[160,16]{1,0:T(8,128)(2,1)S(1)}, u32[]{:S(2)}, u32[]{:S(2)}) collective-permute-start(bf16[160,16]{1,0:T(8,128)(2,1)S(1)} %get-tuple-element.12), channel_id=1, source_target_pairs={{0,1},{1,2},{2,3},{3,4},{4,5},{5,6},{6,7},{8,9},{9,10},{10,11},{11... | collective-permute-start | bytes 15368 | tf_op jit(solution)/shard_map/ppermute | solution.py:19
  108.4 5.3 %collective-permute-start.5 = (bf16[160,16]{1,0:T(8,128)(2,1)S(1)}, bf16[160,16]{1,0:T(8,128)(2,1)S(1)}, u32[]{:S(2)}, u32[]{:S(2)}) collective-permute-start(bf16[160,16]{1,0:T(8,128)(2,1)S(1)} %get-tuple-element.11), channel_id=1, source_target_pairs={{1,0},{2,1},{3,2},{4,3},{5,4},{6,5},{7,6},{9,8},{10,9},{11,10},{12... | collective-permute-start | bytes 15368 | tf_op jit(solution)/shard_map/ppermute | solution.py:20
where the time goes:
time: 139 us; the launch traced here: 138 us
  waiting for transfers between devices  33.5 us (24%)
  other arithmetic  31.6 us (23%)
  matrix products  31.6 us (23%)
  starting transfers between devices  26.9 us (19%)
  local copies, waits for them, and re-layouts  12.3 us (9%)
  between operations  2.25 us (2%)
    all_to_all x1, waiting for transfers between devices, on_device(): lax.all_to_all(send_pixels.reshape(owner_count, capacity, BLOCK_ROWS * BL...  27 us
    select_n x2, other arithmetic, band_matrix(): matrix = jnp.where(lag_index == position, weights[position], matrix)  24.7 us
    dot_general x1, matrix products, on_device(): jnp.dot(row_filter, framed, preferred_element_type=jnp.float32)  21.2 us
    ppermute x3, starting transfers between devices, extended_2(): before = lax.ppermute(last, axis, up)  9.3 us
    ppermute x3, waiting for transfers between devices, extended_2(): after = lax.ppermute(first, axis, down)  6.48 us
    all_to_all x1, starting transfers between devices, on_device(): lax.all_to_all(send_weights.reshape(owner_count, capacity, block_count),...  6.14 us
    all_to_all x1, starting transfers between devices, on_device(): lax.all_to_all(send_pixels.reshape(owner_count, capacity, BLOCK_ROWS * BL...  5.84 us
    ppermute x3, starting transfers between devices, extended_2(): after = lax.ppermute(first, axis, down)  5.62 us
  transfers between devices with their start and end apart: 8, of which 3 were waited for; matrix products, arithmetic and copies ran while one was open for 35% of the time, Pallas kernels for 0%

commit v1 on v0

v1 whole, which is shorter than its diff:
```python
import functools

import jax
import jax.numpy as jnp
from jax import lax
from jax.experimental import pallas as pl
from jax.experimental.pallas import tpu as pltpu
from jax.sharding import Mesh, PartitionSpec as P

BLOCK_ROWS = 32
BLOCK_COLS = 128
MARGIN = 40
HALF_KERNEL = 16
LANES = 128
WIDE = 256
GROUP = 16
F32 = jnp.float32
BF16 = jnp.bfloat16
VMEM = pl.BlockSpec(memory_space=pltpu.VMEM)
SMEM = pl.BlockSpec(memory_space=pltpu.SMEM)


def dot(a, b):
    return jnp.dot(a, b, preferred_element_type=F32)


def iota(shape, axis):
    return lax.broadcasted_iota(jnp.int32, shape, axis)


def shaped(*shape, dtype=BF16):
    return jax.ShapeDtypeStruct(shape, dtype)


def cost(flops, moved):
    return pl.CostEstimate(flops=flops, bytes_accessed=moved, transcendentals=0)


def sinc(x):
    angle = jnp.pi * x
    safe = jnp.where(angle == 0.0, 1.0, angle)
    return jnp.where(angle == 0.0, 1.0, jnp.sin(safe) / safe)


def lanczos_taps(part):
    tap = iota((1, LANES), 1)
    distance = 3.0 - tap.astype(F32) - part
    kernel = jnp.where(tap < 6, sinc(distance) * sinc(distance / 3.0), 0.0)
    kernel = (kernel / jnp.sum(kernel, axis=1, keepdims=True)).astype(BF16).astype(F32)
    return [jnp.sum(jnp.where(tap == k, kernel, 0.0), axis=1, keepdims=True) for k in range(6)]


def band(lag, taps):
    matrix = jnp.zeros(lag.shape, F32)
    for k, tap in enumerate(taps):
        matrix = jnp.where(lag == k, tap, matrix)
    return matrix.astype(BF16)


def warp_matrices_kernel(offset_ref, part_ref, before_ref, own_ref, after_ref, column_ref):
    rows = own_ref.shape[0]
    row_taps = lanczos_taps(part_ref[0])
    first = MARGIN - 3 - offset_ref[0]
    for ref, start in ((before_ref, 0), (own_ref, MARGIN), (after_ref, MARGIN + rows)):
        lag = iota(ref.shape, 1) - iota(ref.shape, 0) + (start - first)
        ref[...] = band(lag, row_taps)
    column_taps = lanczos_taps(part_ref[1])
    lag = iota(column_ref.shape, 0) - iota(column_ref.shape, 1) - (LANES - 3 - offset_ref[1])
    column_ref[...] = band(lag, column_taps)


def warp_matrices(offset, part, rows):
    return pl.pallas_call(
        warp_matrices_kernel,
        out_shape=(
            shaped(rows, MARGIN),
            shaped(rows, rows),
            shaped(rows, MARGIN),
            shaped(WIDE + 2 * LANES, WIDE),
        ),
        in_specs=[SMEM, SMEM],
        out_specs=(VMEM,) * 4,
        cost_estimate=cost(2_000_000, 400_000),
        name="warp_matrices",
    )(offset, part)


def warp_kernel(
    pixel_ref, before_ref, after_ref, row_b_ref, row_o_ref, row_a_ref, column_ref, out_ref,
    padded, ordered,
):
    rows, columns = pixel_ref.shape
    blocks = (rows // BLOCK_ROWS) * (columns // BLOCK_COLS)
    across = columns // BLOCK_COLS
    padded[:, :LANES] = jnp.zeros((rows, LANES), BF16)
    padded[:, LANES + columns :] = jnp.zeros((rows, LANES), BF16)
    step = 2 * WIDE
    for start in range(0, columns, step):
        where = slice(start, start + step)
        summed = dot(row_o_ref[...], pixel_ref[:, where])
        summed += dot(row_b_ref[...], before_ref[:, where])
        summed += dot(row_a_ref[...], after_ref[:, where])
        padded[:, LANES + start : LANES + start + step] = summed.astype(BF16)
    for start in range(0, columns, WIDE):
        warped = dot(padded[:, start : start + WIDE + 2 * LANES], column_ref[...])
        for piece in range(WIDE // BLOCK_COLS):
            j = start // BLOCK_COLS + piece
            for i in range(rows // BLOCK_ROWS):
                ordered[pl.ds(i * across + j, BLOCK_ROWS, stride=blocks), :] = warped[
                    i * BLOCK_ROWS : (i + 1) * BLOCK_ROWS,
                    piece * BLOCK_COLS : (piece + 1) * BLOCK_COLS,
                ]
    out_ref[...] = ordered[...].astype(BF16)


def warp(pixels, before, after, matrices):
    rows, columns = pixels.shape
    total = rows * columns // BLOCK_COLS
    return pl.pallas_call(
        warp_kernel,
        out_shape=shaped(total, BLOCK_COLS),
        in_specs=[VMEM] * 7,
        out_specs=VMEM,
        scratch_shapes=[
            pltpu.VMEM((rows, columns + 2 * LANES), BF16),
            pltpu.VMEM((total, BLOCK_COLS), F32),
        ],
        cost_estimate=cost(700_000_000, 4_000_000),
        name="warp",
    )(pixels, before, after, *matrices)


def route_kernel(
    here_ref, table_ref, place_ref, tag_ref, *, owners_across, dests, capacity, tag_rows, tag_each
):
    blocks = table_ref.shape[1]
    half_across = owners_across // 2
    patch_l = jnp.broadcast_to(table_ref[0:1, :], (blocks, blocks))
    slot_l = jnp.broadcast_to(table_ref[1:2, :], (blocks, blocks))
    weight_l = jnp.broadcast_to(table_ref[2:3, :], (blocks, blocks))
    down, along = iota((blocks, blocks), 0), iota((blocks, blocks), 1)

    def upright(rows):
        return jnp.sum(jnp.where(down == along, rows, 0.0), axis=1, keepdims=True)

    patch_s = upright(patch_l)
    same = (patch_s == patch_l).astype(F32)
    rank_l = jnp.sum(jnp.where(down < along, same, 0.0), axis=0, keepdims=True)
    rank_s = jnp.sum(jnp.where(along < down, same, 0.0), axis=1, keepdims=True)
    patch = table_ref[0:1, :].astype(jnp.int32)
    visit = lax.div(patch, jnp.int32(owners_across))
    column = patch - visit * owners_across - here_ref[0] * half_across
    inside = (column >= 0) & (column < half_across)
    dest = jnp.where(inside, visit * half_across + column, -1)
    rank = rank_l.astype(jnp.int32)

    together = GROUP // capacity
    rows = iota(place_ref.shape[:1] + (blocks,), 0)
    row_dest = lax.div(rows, jnp.int32(GROUP))
    row_in = rows - row_dest * GROUP
    row_part = lax.div(row_in, jnp.int32(capacity))
    hit = (row_dest == dest) & (row_in - row_part * capacity == rank)
    place_ref[...] = jnp.concatenate(
        [(hit & (row_part == part)).astype(F32) for part in range(together)], axis=1
    ).astype(BF16)

    kinds = 2 * tag_each
    rows = iota((dests * tag_rows, blocks), 0)
    row_dest = lax.div(rows, jnp.int32(tag_rows))
    row_kind = rows - row_dest * tag_rows
    left = jnp.concatenate(
        [((row_dest == dest) & (row_kind == kind)).astype(F32) for kind in range(kinds)], axis=1
    ).astype(BF16)
    lane = iota((blocks, LANES), 1)
    pieces = []
    for kind in range(kinds):
        number = lane + (kind % tag_each) * LANES
        source = lax.div(number, jnp.int32(GROUP))
        turn = lax.rem(number, jnp.int32(capacity))
        match = (source == here_ref[1]) & (turn == rank_s.astype(jnp.int32))
        value = upright(slot_l if kind < tag_each else weight_l)
        pieces.append(jnp.where(match, value, 0.0))
    right = jnp.concatenate(pieces, axis=0).astype(BF16)
    tag_ref[...] = dot(left, right).astype(BF16)


def route(here, table, sizes):
    owners_across, dests, capacity, tag_rows, tag_each = sizes
    blocks = table.shape[1]
    body = functools.partial(
        route_kernel,
        owners_across=owners_across,
        dests=dests,
        capacity=capacity,
        tag_rows=tag_rows,
        tag_each=tag_each,
    )
    return pl.pallas_call(
        body,
        out_shape=(
            shaped(dests * GROUP, GROUP // capacity * blocks),
            shaped(dests * tag_rows, LANES),
        ),
        in_specs=[SMEM, VMEM],
        out_specs=(VMEM, VMEM),
        cost_estimate=cost(4_000_000, 200_000),
        name="route",
    )(here, table)


def place_kernel(block_ref, place_ref, tag_ref, out_ref):
    dests, rows, _ = out_ref.shape
    depth = place_ref.shape[1]
    groups = block_ref.shape[0] // depth
    placing = place_ref[...]
    for group in range(0, groups, 2):
        pair = jnp.concatenate(
            [block_ref[(group + n) * depth : (group + n + 1) * depth, :] for n in range(2)], axis=1
        )
        placed = dot(placing, pair).astype(BF16)
        for n in range(2):
            out_ref[:, (group + n) * GROUP : (group + n + 1) * GROUP, :] = placed[
                :, n * LANES : (n + 1) * LANES
            ].reshape(dests, GROUP, LANES)
    tags = rows - groups * GROUP
    out_ref[:, groups * GROUP :, :] = tag_ref[...].reshape(dests, tags, LANES)


def place(blocks, placing, tags):
    dests = placing.shape[0] // GROUP
    rows = blocks.shape[0] // placing.shape[1] * GROUP + tags.shape[0] // dests
    return pl.pallas_call(
        place_kernel,
        out_shape=shaped(dests, rows, LANES),
        in_specs=[VMEM] * 3,
        out_specs=VMEM,
        cost_estimate=cost(300_000_000, 2_000_000),
        name="place",
    )(blocks, placing, tags)


def coadd_kernel(*refs, tag_rows, tag_each, capacity, slots):
    *got_refs, out_ref, top_ref, bottom_ref, ordered = refs
    sources, rows, _ = got_refs[0].shape
    together = GROUP // capacity
    groups = (rows - tag_rows) // GROUP
    across = out_ref.shape[1] // BLOCK_COLS
    weights, total = [], 0.0
    depth = sources * GROUP
    for got in got_refs:
        tags = jnp.sum(got[:, rows - tag_rows :, :].astype(F32), axis=0)
        slot = jnp.concatenate([tags[n : n + 1] for n in range(tag_each)], axis=1)
        weight = jnp.concatenate([tags[tag_each + n : tag_each + n + 1] for n in range(tag_each)], axis=1)
        shape = (together * slots, depth)
        row, lane = iota(shape, 0), iota(shape, 1)
        part = lax.div(row, jnp.int32(slots))
        lane_part = lax.div(lax.rem(lane, jnp.int32(GROUP)), jnp.int32(capacity))
        match = ((row - part * slots) == slot.astype(jnp.int32)) & (part == lane_part)
        matrix = jnp.where(match, weight, 0.0)
        total = total + jnp.sum(matrix, axis=1, keepdims=True)
        weights.append(matrix.astype(BF16))
    divisor = jnp.maximum(total, 1.0)
    for group in range(0, groups, 2):
        summed = 0.0
        for got, matrix in zip(got_refs, weights):
            pair = jnp.concatenate(
                [
                    got[:, (group + n) * GROUP : (group + n + 1) * GROUP, :].reshape(depth, LANES)
                    for n in range(2)
                ],
                axis=1,
            )
            summed = summed + dot(matrix, pair)
        value = summed / divisor
        for n in range(2):
            for part in range(together):
                r = (group + n) * together + part
                ordered[pl.ds(r, slots, stride=BLOCK_ROWS), :] = value[
                    part * slots : (part + 1) * slots, n * LANES : (n + 1) * LANES
                ]
    for q in range(slots):
        y, x = q // across * BLOCK_ROWS, q % across * BLOCK_COLS
        out_ref[y : y + BLOCK_ROWS, x : x + BLOCK_COLS] = ordered[
            q * BLOCK_ROWS : (q + 1) * BLOCK_ROWS, :
        ].astype(BF16)
    patch_rows = out_ref.shape[0]
    top_ref[...] = out_ref[:HALF_KERNEL, :]
    bottom_ref[...] = out_ref[patch_rows - HALF_KERNEL :, :]


def coadd(gots, patch, sizes, slots):
    _, _, capacity, tag_rows, tag_each = sizes
    body = functools.partial(
        coadd_kernel, tag_rows=tag_rows, tag_each=tag_each, capacity=capacity, slots=slots
    )
    return pl.pallas_call(
        body,
        out_shape=(shaped(*patch), shaped(HALF_KERNEL, patch[1]), shaped(HALF_KERNEL, patch[1])),
        in_specs=[VMEM] * len(gots),
        out_specs=(VMEM,) * 3,
        scratch_shapes=[pltpu.VMEM((slots * BLOCK_ROWS, BLOCK_COLS), F32)],
        cost_estimate=cost(600_000_000, 4_000_000),
        name="coadd",
    )(*gots)


def filters_kernel(row_taps_ref, column_taps_ref, top_ref, own_ref, bottom_ref, column_ref):
    rows = own_ref.shape[0]
    taps = [row_taps_ref[k] for k in range(row_taps_ref.shape[0])]
    for ref, start in ((top_ref, 0), (own_ref, HALF_KERNEL), (bottom_ref, HALF_KERNEL + rows)):
        ref[...] = band(iota(ref.shape, 1) - iota(ref.shape, 0) + start, taps)
    taps = [column_taps_ref[k] for k in range(column_taps_ref.shape[0])]
    lag = iota(column_ref.shape, 0) - iota(column_ref.shape, 1) - (LANES - HALF_KERNEL)
    column_ref[...] = band(lag, taps)


def filters(row_taps, column_taps, patch_rows):
    return pl.pallas_call(
        filters_kernel,
        out_shape=(
            shaped(patch_rows, HALF_KERNEL),
            shaped(patch_rows, patch_rows),
            shaped(patch_rows, HALF_KERNEL),
            shaped(WIDE + 2 * LANES, WIDE),
        ),
        in_specs=[SMEM, SMEM],
        out_specs=(VMEM,) * 4,
        cost_estimate=cost(10_000_000, 400_000),
        name="filters",
    )(row_taps, column_taps)


def match_kernel(
    own_ref, above_ref, below_ref, row_t_ref, row_o_ref, row_b_ref, column_ref, out_ref, padded
):
    rows, columns = own_ref.shape
    padded[:, :LANES] = jnp.zeros((rows, LANES), BF16)
    padded[:, LANES + columns :] = jnp.zeros((rows, LANES), BF16)
    step = 2 * WIDE
    for start in range(0, columns, step):
        where = slice(start, start + step)
        summed = dot(row_o_ref[...], own_ref[:, where])
        summed += dot(row_t_ref[...], above_ref[:, where])
        summed += dot(row_b_ref[...], below_ref[:, where])
        padded[:, LANES + start : LANES + start + step] = summed.astype(BF16)
    for start in range(0, columns, WIDE):
        out_ref[:, start : start + WIDE] = dot(
            padded[:, start : start + WIDE + 2 * LANES], column_ref[...]
        )


def match(coadded, above, below, filter_set):
    rows, columns = coadded.shape
    return pl.pallas_call(
        match_kernel,
        out_shape=shaped(rows, columns, dtype=F32),
        in_specs=[VMEM] * 7,
        out_specs=VMEM,
        scratch_shapes=[pltpu.VMEM((rows, columns + 2 * LANES), BF16)],
        cost_estimate=cost(700_000_000, 4_000_000),
        name="match",
    )(coadded, above, below, *filter_set)


def edge_kernel(frame_ref, row_t_ref, row_o_ref, row_b_ref, column_ref, matched_ref, out_ref):
    frame = frame_ref[0]
    rows = row_o_ref.shape[0]
    smoothed = dot(row_o_ref[...], frame[HALF_KERNEL : HALF_KERNEL + rows])
    smoothed += dot(row_t_ref[...], frame[:HALF_KERNEL])
    smoothed += dot(row_b_ref[...], frame[HALF_KERNEL + rows :])
    out_ref[...] = matched_ref[...] + dot(smoothed.astype(BF16), column_ref[...])


def add_edges(matched, frames, filter_set):
    rows, columns = matched.shape
    last = columns // LANES - 1
    row_t, row_o, row_b, column = filter_set
    depth = column.shape[0] // LANES - 1

    def whole(array):
        return pl.BlockSpec(array.shape, lambda side: (0, 0))

    edge = pl.BlockSpec((rows, LANES), lambda side: (0, side * last))
    return pl.pallas_call(
        edge_kernel,
        grid=(2,),
        out_shape=shaped(rows, columns, dtype=F32),
        in_specs=[
            pl.BlockSpec((1,) + frames.shape[1:], lambda side: (side, 0, 0)),
            whole(row_t),
            whole(row_o),
            whole(row_b),
            pl.BlockSpec((LANES, LANES), lambda side: (side * depth, side)),
            edge,
        ],
        out_specs=edge,
        input_output_aliases={5: 0},
        cost_estimate=cost(30_000_000, 300_000),
        name="edges",
    )(frames, row_t, row_o, row_b, column, matched)


def neighbours(x_up, x_down, axis):
    devices = 1
    for name in axis:
        devices *= lax.axis_size(name)
    up = [(i, i + 1) for i in range(devices - 1)]
    down = [(j, i) for i, j in up]
    return lax.ppermute(x_up, axis, up), lax.ppermute(x_down, axis, down)


def on_device(
    exposure, offsets, fraction, route_patch, route_slot, block_weight, kernel_rows, kernel_columns
):
    pixels = exposure[0]
    rows, columns = pixels.shape
    across = ("half", "rest")
    before, after = neighbours(pixels[rows - MARGIN :], pixels[:MARGIN], across)

    blocks = route_patch.shape[1]
    visits, halves, rest = (lax.axis_size(name) for name in ("visit", "half", "rest"))
    owners_across = halves * rest
    dests = visits * rest
    capacity = 4 * blocks // (visits * owners_across)
    tag_each = dests * GROUP // LANES
    tag_rows = max(8, 2 * tag_each)
    sizes = (owners_across, dests, capacity, tag_rows, tag_each)
    table = jnp.concatenate(
        [route_patch.astype(F32), route_slot.astype(F32), block_weight.astype(F32)], axis=0
    )
    swap = [(i, halves - 1 - i) for i in range(halves)]
    other_table = lax.ppermute(table, "half", swap)
    here = jnp.stack(
        [lax.axis_index("half"), lax.axis_index("visit") * rest + lax.axis_index("rest")]
    ).astype(jnp.int32)
    matrices = warp_matrices(offsets.reshape(-1), fraction.reshape(-1), rows)
    placing, tags = route(here, table, sizes)

    warped = warp(pixels, before, after, matrices)
    other_warped = lax.ppermute(warped, "half", swap)
    group = ("visit", "rest")
    own_got = lax.all_to_all(place(warped, placing, tags), group, 0, 0, tiled=True)
    other_placing, other_tags = route(here, other_table, sizes)
    filter_set = filters(kernel_rows, kernel_columns, 2 * rows)
    other_got = lax.all_to_all(
        place(other_warped, other_placing, other_tags), group, 0, 0, tiled=True
    )
    patch = (2 * rows, columns // 2)
    coadded, top, bottom = coadd((own_got, other_got), patch, sizes, blocks)

    above, below = neighbours(bottom, top, ("visit",))
    ends = [
        jnp.concatenate([above[:, s], coadded[:, s], below[:, s]], axis=0)
        for s in (slice(patch[1] - LANES, patch[1]), slice(0, LANES))
    ]
    matched = match(coadded, above, below, filter_set)
    frames = jnp.stack(neighbours(ends[0], ends[1], across))
    matched = add_edges(matched, frames, filter_set)
    return (coadded, matched)


def solution(mesh):
    visits, ccds = (mesh.shape[name] for name in ("visit", "ccd"))
    split = Mesh(mesh.devices.reshape(visits, 2, ccds // 2), ("visit", "half", "rest"))
    ccd = ("half", "rest")
    placed = (
        P("visit", ccd, None),
        P("visit", ccd, None),
        P("visit", ccd, None),
        P("visit", ccd),
        P("visit", ccd),
        P("visit", ccd),
        P(),
        P(),
    )
    return jax.shard_map(
        on_device,
        mesh=split,
        in_specs=placed,
        out_specs=(P("visit", ccd), P("visit", ccd)),
        check_vma=False,
    )
```

time: 139 us -> 104 us (0.75)
  matrix products: 31.6 us -> 0 us
  other arithmetic: 31.6 us -> 1.82 us
  Pallas kernels: 0 us -> 24.6 us
  local copies, waits for them, and re-layouts: 12.3 us -> 5.03 us
  waiting for transfers between devices: 33.5 us -> 40.2 us
  starting transfers between devices: 26.9 us -> 30.5 us
  between operations: 2.25 us -> 0.83 us
    dot_general x11 -> x0, matrix products: 31.6 us -> none  [the longest x1 21.2 us: on_device(): jnp.dot(row_filter, framed, preferred_element_type=jnp.float32)]
    select_n x2 -> x0, other arithmetic: 24.7 us -> none  [band_matrix(): matrix = jnp.where(lag_index == position, weights[position], matrix)]
    pallas_call x0 -> x10, Pallas kernels: none -> 24.6 us  [the longest x2 4.98 us: place(): pl.pallas_call(place_kernel, out_shape=shaped(dests, rows, LANES), in_spe...]
    ppermute x6 -> x8, waiting for transfers between devices: 6.49 us -> 26.7 us  [the longest x1 21.6 us: on_device(): other_table = lax.ppermute(table, 'half', swap)]
    all_to_all x2, waiting for transfers between devices: 27 us -> 13.6 us  [the longest x1 13.6 us: on_device(): lax.all_to_all(place(other_warped, other_placing, other_tags), group, 0,...]
    slice x11 -> x4, local copies, waits for them, and re-layouts: 8.12 us -> 1.93 us  [the longest x1 1.13 us: on_device(): before, after = neighbours(pixels[rows - MARGIN:], pixels[:MARGIN], across)]
    ppermute x6 -> x8, starting transfers between devices: 14.9 us -> 18.8 us  [the longest x6 16.4 us: neighbours(): return (lax.ppermute(x_up, axis, up), lax.ppermute(x_down, axis, down))]
    reduce_sum x4 -> x0, other arithmetic: 3.56 us -> none  [the longest x2 2.61 us: lanczos_weights(): return (kernel / jnp.sum(kernel)).astype(jnp.bfloat16)]
  transfers between devices with their start and end apart: 8 -> 10, of which waited for: 3 -> 5; matrix products, arithmetic and copies ran while one was open for 35% -> 2% of each run, Pallas kernels for 0% -> 13%
where the time goes in v1:
time: 104 us; the launch traced here: 103 us
  waiting for transfers between devices  40.2 us (39%)
  starting transfers between devices  30.5 us (29%)
  Pallas kernels  24.6 us (24%)
  local copies, waits for them, and re-layouts  5.03 us (5%)
  other arithmetic  1.82 us (2%)
    ppermute x1, waiting for transfers between devices, on_device(): other_table = lax.ppermute(table, 'half', swap)  21.6 us
    ppermute x6, starting transfers between devices, neighbours(): return (lax.ppermute(x_up, axis, up), lax.ppermute(x_down, axis, down))  16.4 us
    all_to_all x1, waiting for transfers between devices, on_device(): lax.all_to_all(place(other_warped, other_placing, other_tags), group, 0,...  13.6 us
    all_to_all x1, starting transfers between devices, on_device(): lax.all_to_all(place(other_warped, other_placing, other_tags), group, 0,...  6.66 us
    ppermute x6, waiting for transfers between devices, neighbours(): return (lax.ppermute(x_up, axis, up), lax.ppermute(x_down, axis, down))  5.03 us
    all_to_all x1, starting transfers between devices, on_device(): lax.all_to_all(place(warped, placing, tags), group, 0, 0, tiled=True)  4.99 us
    pallas_call x2, Pallas kernels, place(): pl.pallas_call(place_kernel, out_shape=shaped(dests, rows, LANES), in_spe...  4.98 us
    pallas_call x1, Pallas kernels, warp(): pl.pallas_call(warp_kernel, out_shape=shaped(total, BLOCK_COLS), in_specs...  3.7 us
  transfers between devices with their start and end apart: 10, of which 5 were waited for; matrix products, arithmetic and copies ran while one was open for 2% of the time, Pallas kernels for 13%

profile of v1, /device:TPU:1, one launch (start us, length us, event | category | flops | bytes accessed | tf_op | source)
XLA Modules:
  0.0 103.0 jit_solution(1794745429687038841)
XLA Ops:
  0.6 0.0 copy-start.10
  0.6 0.0 copy-start.11
  0.7 0.0 copy-start.12
  0.7 1.1 %slice_bitcast_fusion = (bf16[40,4096]{1,0:T(8,128)(2,1)S(1)}, bf16[40,4096]{1,0:T(8,128)(2,1)S(1)}) fusion(bf16[1,64,4096]{2,1,0:T(8,128)(2,1)} %param.8), kind=kLoop, calls=%fused_computation | loop fusion | bytes 1310720 | tf_op jit(solution)/shard_map/slice | solution.py:418
  1.8 4.6 %collective-permute-start = (bf16[40,4096]{1,0:T(8,128)(2,1)S(1)}, bf16[40,4096]{1,0:T(8,128)(2,1)S(1)}, u32[]{:S(2)}, u32[]{:S(2)}) collective-permute-start(bf16[40,4096]{1,0:T(8,128)(2,1)S(1)} %get-tuple-element.35), channel_id=1, source_target_pairs={{0,1},{1,2},{2,3},{3,4},{4,5},{5,6},{6,7},{8,9},{9,10},{10,11},{11... | collective-permute-start | bytes 983048 | tf_op jit(solution)/shard_map/ppermute | solution.py:409
  6.4 1.9 %collective-permute-start.1 = (bf16[40,4096]{1,0:T(8,128)(2,1)S(1)}, bf16[40,4096]{1,0:T(8,128)(2,1)S(1)}, u32[]{:S(2)}, u32[]{:S(2)}) collective-permute-start(bf16[40,4096]{1,0:T(8,128)(2,1)S(1)} %get-tuple-element.34), channel_id=1, source_target_pairs={{1,0},{2,1},{3,2},{4,3},{5,4},{6,5},{7,6},{9,8},{10,9},{11,10},{12... | collective-permute-start | bytes 983048 | tf_op jit(solution)/shard_map/ppermute | solution.py:409
  8.3 0.0 copy-done.10
  8.3 0.0 copy-done.11
  8.4 0.0 copy-done.12
  8.4 2.0 %warp_matrices.1 = (bf16[64,40]{1,0:T(8,128)(2,1)}, bf16[64,64]{1,0:T(8,128)(2,1)}, bf16[64,40]{1,0:T(8,128)(2,1)}, bf16[512,256]{1,0:T(8,128)(2,1)}) custom-call(s32[2]{0:T(128)} %bitcast.14, f32[2]{0:T(128)} %bitcast.15), custom_call_target="tpu_custom_call" | custom-call | flops 2000000 | bytes 400000 | tf_op jit(solution)/shard_map/warp_matrices/pallas_call | solution.py:73
  10.4 0.6 pad_add_fusion.here_ref
  11.0 0.6 pad_maximum_fusion.3.table_ref
  11.6 1.7 %route.2 = (bf16[256,128]{1,0:T(8,128)(2,1)}, bf16[128,128]{1,0:T(8,128)(2,1)}) custom-call(s32[2]{0:T(128)} %pad_add_fusion.here_ref, f32[3,64]{1,0:T(4,128)} %pad_maximum_fusion.3.table_ref), custom_call_target="tpu_custom_call" | custom-call | flops 4000000 | bytes 200000 | tf_op jit(solution)/shard_map/route/pallas_call | solution.py:198
  13.2 0.0 collective-permute-done.before_ref
  13.2 0.0 copy-start.7
  13.2 1.6 %collective-permute-done.1.after_ref = bf16[40,4096]{1,0:T(8,128)(2,1)S(1)} collective-permute-done((bf16[40,4096]{1,0:T(8,128)(2,1)S(1)}, bf16[40,4096]{1,0:T(8,128)(2,1)S(1)}, u32[]{:S(2)}, u32[]{:S(2)}) %collective-permute-start.1) | collective-permute-done | bytes 327712 | tf_op jit(solution)/shard_map/ppermute | solution.py:409
  14.8 0.0 copy-start.8
  14.8 0.0 copy-done.7
  14.8 0.7 copy-done.8
  15.5 3.7 %warp.1.block_ref = bf16[2048,128]{1,0:T(8,128)(2,1)} custom-call(bf16[64,4096]{1,0:T(8,128)(2,1)} %bitcast.11, bf16[40,4096]{1,0:T(8,128)(2,1)} %copy-done.7, bf16[40,4096]{1,0:T(8,128)(2,1)} %copy-done.8, bf16[64,40]{1,0:T(8,128)(2,1)} %get-tuple-element.17.row_b_ref, bf16[64,64]{1,0:T(8,128)(2,1)} %get-tuple-element.18.row_o_ref, ...), custom_call_target="tpu_custom_call" | custom-call | flops 700000000 | bytes 4000000 | tf_op jit(solution)/shard_map/warp/pallas_call | solution.py:119
  19.2 2.5 %place.2 = bf16[16,264,128]{2,1,0:T(8,128)(2,1)} custom-call(bf16[2048,128]{1,0:T(8,128)(2,1)} %warp.1.block_ref, bf16[256,128]{1,0:T(8,128)(2,1)} %get-tuple-element.21.place_ref, bf16[128,128]{1,0:T(8,128)(2,1)} %get-tuple-element.22.tag_ref), custom_call_target="tpu_custom_call" | custom-call | flops 300000000 | bytes 2000000 | tf_op jit(solution)/shard_map/place/pallas_call | solution.py:232
  21.7 0.0 copy-start.2
  21.7 0.0 copy-start.4
  21.7 5.0 %all-to-all-start = ((bf16[16,264,128]{2,1,0:T(8,128)(2,1)}), bf16[16,264,128]{2,1,0:T(8,128)(2,1)S(1)}, u32[]{:S(2)}, u32[]{:S(2)}) async-start(bf16[16,264,128]{2,1,0:T(8,128)(2,1)} %place.2), calls=%async_computation | async-start | bytes 2162688 | tf_op jit(solution)/shard_map/all_to_all | solution.py:442
  26.7 0.0 copy-done.2
  26.7 1.4 %collective-permute-start.2 = (bf16[2048,128]{1,0:T(8,128)(2,1)S(1)}, bf16[2048,128]{1,0:T(8,128)(2,1)S(1)}, u32[]{:S(2)}, u32[]{:S(2)}) collective-permute-start(bf16[2048,128]{1,0:T(8,128)(2,1)S(1)} %copy-done.2), channel_id=1, source_target_pairs={{0,4},{4,0},{1,5},{5,1},{2,6},{6,2},{3,7},{7,3},{8,12},{12,8},{9,1... | collective-permute-start | bytes 1572872 | tf_op jit(solution)/shard_map/ppermute | solution.py:440
  28.1 0.0 copy-done.4
  28.1 1.1 %collective-permute-start.3 = (f32[3,64]{1,0:T(4,128)S(1)}, f32[3,64]{1,0:T(4,128)S(1)}, u32[]{:S(2)}, u32[]{:S(2)}) collective-permute-start(f32[3,64]{1,0:T(4,128)S(1)} %copy-done.4), channel_id=1, source_target_pairs={{0,4},{4,0},{1,5},{5,1},{2,6},{6,2},{3,7},{7,3},{8,12},{12,8},{9,1... | collective-permute-start | bytes 2312 | tf_op jit(solution)/shard_map/ppermute | solution.py:432
  29.1 21.6 %collective-permute-done.3.table_ref = f32[3,64]{1,0:T(4,128)S(1)} collective-permute-done((f32[3,64]{1,0:T(4,128)S(1)}, f32[3,64]{1,0:T(4,128)S(1)}, u32[]{:S(2)}, u32[]{:S(2)}) %collective-permute-start.3) | collective-permute-done | bytes 800 | tf_op jit(solution)/shard_map/ppermute | solution.py:432
  50.8 0.0 copy-start.9
  50.8 0.6 copy-done.9
  51.3 1.7 %route.3 = (bf16[256,128]{1,0:T(8,128)(2,1)}, bf16[128,128]{1,0:T(8,128)(2,1)}) custom-call(s32[2]{0:T(128)} %pad_add_fusion.here_ref, f32[3,64]{1,0:T(4,128)} %copy-done.9), custom_call_target="tpu_custom_call" | custom-call | flops 4000000 | bytes 200000 | tf_op jit(solution)/shard_map/route/pallas_call | solution.py:198
  53.0 0.0 collective-permute-done.2.block_ref
  53.0 0.0 copy-start.3
  53.0 0.8 copy-done.3
  53.8 2.5 %place.3 = bf16[16,264,128]{2,1,0:T(8,128)(2,1)} custom-call(bf16[2048,128]{1,0:T(8,128)(2,1)} %copy-done.3, bf16[256,128]{1,0:T(8,128)(2,1)} %get-tuple-element.23.place_ref, bf16[128,128]{1,0:T(8,128)(2,1)} %get-tuple-element.24.tag_ref), custom_call_target="tpu_custom_call" | custom-call | flops 300000000 | bytes 2000000 | tf_op jit(solution)/shard_map/place/pallas_call | solution.py:232
  56.3 0.0 all-to-all-done.refs_0_
  56.3 0.0 copy-start
  56.3 6.7 %all-to-all-start.1 = ((bf16[16,264,128]{2,1,0:T(8,128)(2,1)}), bf16[16,264,128]{2,1,0:T(8,128)(2,1)S(1)}, u32[]{:S(2)}, u32[]{:S(2)}) async-start(bf16[16,264,128]{2,1,0:T(8,128)(2,1)} %place.3), calls=%async_computation.1 | async-start | bytes 2162688 | tf_op jit(solution)/shard_map/all_to_all | solution.py:445
  63.0 2.1 %filters.1 = (bf16[128,16]{1,0:T(8,128)(2,1)}, bf16[128,128]{1,0:T(8,128)(2,1)}, bf16[128,16]{1,0:T(8,128)(2,1)}, bf16[512,256]{1,0:T(8,128)(2,1)}) custom-call(f32[33]{0:T(128)} %row_taps_ref.1, f32[33]{0:T(128)} %column_taps_ref.1), custom_call_target="tpu_custom_call" | custom-call | flops 10000000 | bytes 400000 | tf_op jit(solution)/shard_map/filters/pallas_call | solution.py:318
  65.0 0.0 copy-done
  65.0 13.6 %all-to-all-done.1.refs_1_ = bf16[16,264,128]{2,1,0:T(8,128)(2,1)S(1)} async-done(((bf16[16,264,128]{2,1,0:T(8,128)(2,1)}), bf16[16,264,128]{2,1,0:T(8,128)(2,1)S(1)}, u32[]{:S(2)}, u32[]{:S(2)}) %all-to-all-start.1) | async-done | bytes 1081376 | tf_op jit(solution)/shard_map/all_to_all | solution.py:445
  78.6 0.0 copy-start.1
  78.6 1.0 copy-done.1
  79.6 3.4 %coadd.1 = (bf16[128,2048]{1,0:T(8,128)(2,1)}, bf16[16,2048]{1,0:T(8,128)(2,1)}, bf16[16,2048]{1,0:T(8,128)(2,1)}) custom-call(bf16[16,264,128]{2,1,0:T(8,128)(2,1)} %copy-done, bf16[16,264,128]{2,1,0:T(8,128)(2,1)} %copy-done.1), custom_call_target="tpu_custom_call" | custom-call | flops 600000000 | bytes 4000000 | tf_op jit(solution)/shard_map/coadd/pallas_call | solution.py:296
  83.0 2.5 %collective-permute-start.4 = (bf16[16,2048]{1,0:T(8,128)(2,1)}, bf16[16,2048]{1,0:T(8,128)(2,1)S(1)}, u32[]{:S(2)}, u32[]{:S(2)}) collective-permute-start(bf16[16,2048]{1,0:T(8,128)(2,1)} %get-tuple-element.26), channel_id=1, source_target_pairs={{0,8},{8,16},{16,24},{1,9},{9,17},{17,25},{2,10},{10,18},{18,26},{... | collective-permute-start | bytes 196616 | tf_op jit(solution)/shard_map/ppermute | solution.py:409
  85.5 1.3 %collective-permute-start.5 = (bf16[16,2048]{1,0:T(8,128)(2,1)}, bf16[16,2048]{1,0:T(8,128)(2,1)S(1)}, u32[]{:S(2)}, u32[]{:S(2)}) collective-permute-start(bf16[16,2048]{1,0:T(8,128)(2,1)} %get-tuple-element.27), channel_id=1, source_target_pairs={{8,0},{16,8},{24,16},{9,1},{17,9},{25,17},{10,2},{18,10},{26,18},{... | collective-permute-start | bytes 196616 | tf_op jit(solution)/shard_map/ppermute | solution.py:409
  86.8 0.8 fusion
  87.6 0.0 collective-permute-done.4.above_ref
  87.6 0.0 copy-start.5
  87.6 3.1 %collective-permute-done.5.below_ref = bf16[16,2048]{1,0:T(8,128)(2,1)S(1)} collective-permute-done((bf16[16,2048]{1,0:T(8,128)(2,1)}, bf16[16,2048]{1,0:T(8,128)(2,1)S(1)}, u32[]{:S(2)}, u32[]{:S(2)}) %collective-permute-start.5) | collective-permute-done | bytes 65568 | tf_op jit(solution)/shard_map/ppermute | solution.py:409
  90.7 0.0 copy-start.6
  90.7 4.1 %collective-permute-start.6 = (bf16[160,128]{1,0:T(8,128)(2,1)S(1)}, bf16[160,128]{1,0:T(8,128)(2,1)S(1)}, u32[]{:S(2)}, u32[]{:S(2)}) collective-permute-start(bf16[160,128]{1,0:T(8,128)(2,1)S(1)} %pad_maximum_fusion.1), channel_id=1, source_target_pairs={{0,1},{1,2},{2,3},{3,4},{4,5},{5,6},{6,7},{8,9},{9,10},{10,11},{11... | collective-permute-start | bytes 122888 | tf_op jit(solution)/shard_map/ppermute | solution.py:409
  94.9 1.9 %collective-permute-start.7 = (bf16[160,128]{1,0:T(8,128)(2,1)S(1)}, bf16[160,128]{1,0:T(8,128)(2,1)S(1)}, u32[]{:S(2)}, u32[]{:S(2)}) collective-permute-start(bf16[160,128]{1,0:T(8,128)(2,1)S(1)} %pad_maximum_fusion.2), channel_id=1, source_target_pairs={{1,0},{2,1},{3,2},{4,3},{5,4},{6,5},{7,6},{9,8},{10,9},{11,10},{12... | collective-permute-start | bytes 122888 | tf_op jit(solution)/shard_map/ppermute | solution.py:409
  96.8 0.0 copy-done.5
  96.8 0.0 copy-done.6
  96.8 3.0 %match.1.matched_ref = f32[128,2048]{1,0:T(8,128)} custom-call(bf16[128,2048]{1,0:T(8,128)(2,1)} %get-tuple-element.15.own_ref, bf16[16,2048]{1,0:T(8,128)(2,1)} %copy-done.5, bf16[16,2048]{1,0:T(8,128)(2,1)} %copy-done.6, bf16[128,16]{1,0:T(8,128)(2,1)} %get-tuple-element.28.row_t_ref, bf16[128,128]{1,0:T(8,128)(2,1)} %get-tuple-element.29.row_o_ref, ...), custom_call_target="tpu_custom_call" | custom-call | flops 700000000 | bytes 4000000 | tf_op jit(solution)/shard_map/match/pallas_call | solution.py:354
  99.8 0.0 collective-permute-done.6
  99.8 0.4 collective-permute-done.7
  100.2 0.6 pad_maximum_fusion.frame_ref
  100.8 2.1 %edges.1 = f32[128,2048]{1,0:T(8,128)} custom-call(bf16[2,160,128]{2,1,0:T(8,128)(2,1)} %pad_maximum_fusion.frame_ref, bf16[128,16]{1,0:T(8,128)(2,1)} %get-tuple-element.28.row_t_ref, bf16[128,128]{1,0:T(8,128)(2,1)} %get-tuple-element.29.row_o_ref, bf16[128,16]{1,0:T(8,128)(2,1)} %get-tuple-element.30.row_b_ref, ...), custom_call_target="tpu_custom_call", output_to_operand_aliasing={{}: (5, {})} | custom-call | flops 30000000 | bytes 300000 | tf_op jit(solution)/shard_map/edges/pallas_call | solution.py:384
  (7 shorter events, 0.0 us)
Async XLA Ops:
  0.6 7.7 %copy-start.10 = (s32[1,64]{1,0:T(1,128)S(1)}, s32[1,64]{1,0:T(1,128)}, u32[]{:S(2)}) copy-start(s32[1,64]{1,0:T(1,128)} %param.12) | copy-start | bytes 772
  0.6 7.7 %copy-start.11 = (bf16[1,64]{1,0:T(2,128)(2,1)S(1)}, bf16[1,64]{1,0:T(2,128)(2,1)}, u32[]{:S(2)}) copy-start(bf16[1,64]{1,0:T(2,128)(2,1)} %param.13) | copy-start | bytes 388
  0.7 7.7 %copy-start.12 = (s32[1,64]{1,0:T(1,128)S(1)}, s32[1,64]{1,0:T(1,128)}, u32[]{:S(2)}) copy-start(s32[1,64]{1,0:T(1,128)} %param.11) | copy-start | bytes 772
  1.8 11.4 %collective-permute-start = (bf16[40,4096]{1,0:T(8,128)(2,1)S(1)}, bf16[40,4096]{1,0:T(8,128)(2,1)S(1)}, u32[]{:S(2)}, u32[]{:S(2)}) collective-permute-start(bf16[40,4096]{1,0:T(8,128)(2,1)S(1)} %get-tuple-element.35), channel_id=1, source_target_pairs={{0,1},{1,2},{2,3},{3,4},{4,5},{5,6},{6,7},{8,9},{9,10},{10,11},{11... | collective-permute-start | bytes 983048 | tf_op jit(solution)/shard_map/ppermute | solution.py:409
  6.4 8.4 %collective-permute-start.1 = (bf16[40,4096]{1,0:T(8,128)(2,1)S(1)}, bf16[40,4096]{1,0:T(8,128)(2,1)S(1)}, u32[]{:S(2)}, u32[]{:S(2)}) collective-permute-start(bf16[40,4096]{1,0:T(8,128)(2,1)S(1)} %get-tuple-element.34), channel_id=1, source_target_pairs={{1,0},{2,1},{3,2},{4,3},{5,4},{6,5},{7,6},{9,8},{10,9},{11,10},{12... | collective-permute-start | bytes 983048 | tf_op jit(solution)/shard_map/ppermute | solution.py:409
  13.2 1.6 %copy-start.7 = (bf16[40,4096]{1,0:T(8,128)(2,1)}, bf16[40,4096]{1,0:T(8,128)(2,1)S(1)}, u32[]{:S(2)}) copy-start(bf16[40,4096]{1,0:T(8,128)(2,1)S(1)} %collective-permute-done.before_ref) | copy-start | bytes 983044
  14.8 0.7 copy-start.8
  21.7 5.0 %copy-start.2 = (bf16[2048,128]{1,0:T(8,128)(2,1)S(1)}, bf16[2048,128]{1,0:T(8,128)(2,1)}, u32[]{:S(2)}) copy-start(bf16[2048,128]{1,0:T(8,128)(2,1)} %warp.1.block_ref) | copy-start | bytes 1572868
  21.7 6.4 %copy-start.4 = (f32[3,64]{1,0:T(4,128)S(1)}, f32[3,64]{1,0:T(4,128)}, u32[]{:S(2)}) copy-start(f32[3,64]{1,0:T(4,128)} %pad_maximum_fusion.3.table_ref) | copy-start | bytes 2308
  21.7 34.6 %all-to-all-start = ((bf16[16,264,128]{2,1,0:T(8,128)(2,1)}), bf16[16,264,128]{2,1,0:T(8,128)(2,1)S(1)}, u32[]{:S(2)}, u32[]{:S(2)}) async-start(bf16[16,264,128]{2,1,0:T(8,128)(2,1)} %place.2), calls=%async_computation | async-start | bytes 2162688 | tf_op jit(solution)/shard_map/all_to_all | solution.py:442
  26.7 26.3 %collective-permute-start.2 = (bf16[2048,128]{1,0:T(8,128)(2,1)S(1)}, bf16[2048,128]{1,0:T(8,128)(2,1)S(1)}, u32[]{:S(2)}, u32[]{:S(2)}) collective-permute-start(bf16[2048,128]{1,0:T(8,128)(2,1)S(1)} %copy-done.2), channel_id=1, source_target_pairs={{0,4},{4,0},{1,5},{5,1},{2,6},{6,2},{3,7},{7,3},{8,12},{12,8},{9,1... | collective-permute-start | bytes 1572872 | tf_op jit(solution)/shard_map/ppermute | solution.py:440
  28.1 22.7 %collective-permute-start.3 = (f32[3,64]{1,0:T(4,128)S(1)}, f32[3,64]{1,0:T(4,128)S(1)}, u32[]{:S(2)}, u32[]{:S(2)}) collective-permute-start(f32[3,64]{1,0:T(4,128)S(1)} %copy-done.4), channel_id=1, source_target_pairs={{0,4},{4,0},{1,5},{5,1},{2,6},{6,2},{3,7},{7,3},{8,12},{12,8},{9,1... | collective-permute-start | bytes 2312 | tf_op jit(solution)/shard_map/ppermute | solution.py:432
  50.8 0.6 copy-start.9
  53.0 0.8 copy-start.3
  56.3 8.7 %copy-start = (bf16[16,264,128]{2,1,0:T(8,128)(2,1)}, bf16[16,264,128]{2,1,0:T(8,128)(2,1)S(1)}, u32[]{:S(2)}) copy-start(bf16[16,264,128]{2,1,0:T(8,128)(2,1)S(1)} %all-to-all-done.refs_0_) | copy-start | bytes 3244036
  56.3 22.3 %all-to-all-start.1 = ((bf16[16,264,128]{2,1,0:T(8,128)(2,1)}), bf16[16,264,128]{2,1,0:T(8,128)(2,1)S(1)}, u32[]{:S(2)}, u32[]{:S(2)}) async-start(bf16[16,264,128]{2,1,0:T(8,128)(2,1)} %place.3), calls=%async_computation.1 | async-start | bytes 2162688 | tf_op jit(solution)/shard_map/all_to_all | solution.py:445
  78.6 1.0 copy-start.1
  83.0 4.6 %collective-permute-start.4 = (bf16[16,2048]{1,0:T(8,128)(2,1)}, bf16[16,2048]{1,0:T(8,128)(2,1)S(1)}, u32[]{:S(2)}, u32[]{:S(2)}) collective-permute-start(bf16[16,2048]{1,0:T(8,128)(2,1)} %get-tuple-element.26), channel_id=1, source_target_pairs={{0,8},{8,16},{16,24},{1,9},{9,17},{17,25},{2,10},{10,18},{18,26},{... | collective-permute-start | bytes 196616 | tf_op jit(solution)/shard_map/ppermute | solution.py:409
  85.5 5.2 %collective-permute-start.5 = (bf16[16,2048]{1,0:T(8,128)(2,1)}, bf16[16,2048]{1,0:T(8,128)(2,1)S(1)}, u32[]{:S(2)}, u32[]{:S(2)}) collective-permute-start(bf16[16,2048]{1,0:T(8,128)(2,1)} %get-tuple-element.27), channel_id=1, source_target_pairs={{8,0},{16,8},{24,16},{9,1},{17,9},{25,17},{10,2},{18,10},{26,18},{... | collective-permute-start | bytes 196616 | tf_op jit(solution)/shard_map/ppermute | solution.py:409
  87.6 9.2 %copy-start.5 = (bf16[16,2048]{1,0:T(8,128)(2,1)}, bf16[16,2048]{1,0:T(8,128)(2,1)S(1)}, u32[]{:S(2)}) copy-start(bf16[16,2048]{1,0:T(8,128)(2,1)S(1)} %collective-permute-done.4.above_ref) | copy-start | bytes 196612
  90.7 6.1 %copy-start.6 = (bf16[16,2048]{1,0:T(8,128)(2,1)}, bf16[16,2048]{1,0:T(8,128)(2,1)S(1)}, u32[]{:S(2)}) copy-start(bf16[16,2048]{1,0:T(8,128)(2,1)S(1)} %collective-permute-done.5.below_ref) | copy-start | bytes 196612
  90.7 9.1 %collective-permute-start.6 = (bf16[160,128]{1,0:T(8,128)(2,1)S(1)}, bf16[160,128]{1,0:T(8,128)(2,1)S(1)}, u32[]{:S(2)}, u32[]{:S(2)}) collective-permute-start(bf16[160,128]{1,0:T(8,128)(2,1)S(1)} %pad_maximum_fusion.1), channel_id=1, source_target_pairs={{0,1},{1,2},{2,3},{3,4},{4,5},{5,6},{6,7},{8,9},{9,10},{10,11},{11... | collective-permute-start | bytes 122888 | tf_op jit(solution)/shard_map/ppermute | solution.py:409
  94.9 5.3 %collective-permute-start.7 = (bf16[160,128]{1,0:T(8,128)(2,1)S(1)}, bf16[160,128]{1,0:T(8,128)(2,1)S(1)}, u32[]{:S(2)}, u32[]{:S(2)}) collective-permute-start(bf16[160,128]{1,0:T(8,128)(2,1)S(1)} %pad_maximum_fusion.2), channel_id=1, source_target_pairs={{1,0},{2,1},{3,2},{4,3},{5,4},{6,5},{7,6},{9,8},{10,9},{11,10},{12... | collective-permute-start | bytes 122888 | tf_op jit(solution)/shard_map/ppermute | solution.py:409
